TPU v7x, 512 devices: a whole 4x4x16 slice. The times are simulated.
512 devices in a mesh: tok: 64 (over z_hi, y, x), head: 8 (over z_lo, core).
Axes of the slice: x: 4, y: 4, z: 16 (z_hi: 4, z_lo: 4; z = z_hi * 4 + z_lo), core: 2. Of those that a mesh axis runs over, the one named last changes fastest.
Arguments:
- hidden_in: bfloat16 [16384, 2560], P('tok'), may hold values from -6 to 6
- norm_gain: float32 [2560], replicated, may hold values from 0.1 to 1.9
- w_qkv: bfloat16 [2560, 3840], P('tok', 'head'), may hold values from -4 to 4
- w_out: bfloat16 [2560, 2560], P('head', 'tok'), may hold values from -0.625 to 0.625
- prefill_cache: bfloat16 [8, 4096, 8, 1280], P(None, 'tok', 'head'), may hold values from -6 to 6
- lengths: int32 [8], replicated, may hold values from 1 to 4096, 20480 in all
- prefill_table: int32 [4096], replicated, may hold values from 0 to 4095, as said below
- decode_table: int32 [4096], replicated, may hold values from 0 to 4095, as said below
Outputs:
- attn_out: bfloat16 [16384, 2560], P('tok', 'head')
- decode_cache: bfloat16 [8, 4096, 8, 1280], P(None, 'tok', 'head')
Inputs may be any that keep to these rules, and one draw needn't show every extreme that they name: `prefill_table`: each prefill slot holds exactly one logical block. `decode_table`: the block in prefill slot s * 64 + k goes to decode slot d * 64 + k, where d - s modulo the size of tok depends only on k and each residue occurs for exactly 1 values of k.
All inputs are finite; a program needn't handle non-finite values.
Results may differ from a plain program's by a relative error of at most 0.015.
The roundings to bfloat16 on the way count: a program that leaves them out, or rounds other values in their place, can miss the bound.
Values may be sent and summed in bfloat16 or wider, within the bound.
A program may use at most 64 MiB of HBM per device.

v0:
```python
import math
import jax
import jax.numpy as jnp
from jax import lax
from jax.sharding import PartitionSpec as P

HD = 80
QPK = 4
BLK = 8
NORM_EPS = 1e-05
ROPE_BASE = 1000000.0


def rotary(vectors, positions):
    half_width = vectors.shape[-1] // 2
    frequency = ROPE_BASE ** (-2.0 * jnp.arange(half_width, dtype=jnp.float32) / vectors.shape[-1])
    angles = positions.astype(jnp.float32)[:, None] * frequency[None, :]
    cosine = jnp.cos(angles)[:, None, :]
    sines = jnp.sin(angles)[:, None, :]
    front_half = vectors[..., :half_width]
    back_half = vectors[..., half_width:]
    return jnp.concatenate(
        [front_half * cosine - back_half * sines, back_half * cosine + front_half * sines], axis=-1
    )


def attend(hidden_in, norm_gain, w_qkv):
    tok_rows = hidden_in.shape[0]
    my_index = lax.axis_index("tok")
    float_rows = hidden_in.astype(jnp.float32)
    normed = (
        float_rows
        * lax.rsqrt(jnp.mean(float_rows * float_rows, axis=-1, keepdims=True) + NORM_EPS)
        * norm_gain
    ).astype(jnp.bfloat16)
    projected = jnp.dot(
        normed, lax.all_gather(w_qkv, "tok", axis=0, tiled=True), preferred_element_type=jnp.float32
    )
    kv_local = w_qkv.shape[1] // ((QPK + 2) * HD)
    projected = projected.reshape(tok_rows, kv_local, QPK + 2, HD)
    row_index = jnp.arange(tok_rows, dtype=jnp.int32)
    positions = my_index * tok_rows + row_index
    queries = (
        rotary(projected[:, :, :QPK].reshape(tok_rows, kv_local * QPK, HD), positions)
        .astype(jnp.bfloat16)
        .reshape(tok_rows, kv_local * QPK * HD)
    )
    key_rows = (
        rotary(projected[:, :, QPK], positions)
        .astype(jnp.bfloat16)
        .reshape(tok_rows, kv_local * HD)
    )
    values = projected[:, :, QPK + 1].astype(jnp.bfloat16).reshape(tok_rows, kv_local * HD)
    query_grid = (
        queries.reshape(tok_rows, kv_local, QPK, HD)
        .transpose(1, 2, 0, 3)
        .reshape(kv_local, QPK * tok_rows, HD)
    )
    query_pos = jnp.tile(positions, QPK)
    last_row = jnp.max(positions)
    scale_factor = 1.0 / math.sqrt(HD)

    def key_positions(block_start, count):
        whole_rows = block_start + jnp.arange(count, dtype=jnp.int32)
        return whole_rows

    initial = (
        jnp.full((kv_local, QPK * tok_rows), -1e30, jnp.float32),
        jnp.zeros((kv_local, QPK * tok_rows), jnp.float32),
        jnp.zeros((kv_local, QPK * tok_rows, HD), jnp.float32),
    )
    key_part = lax.all_gather(key_rows, "tok", axis=0, tiled=True)
    value_part = lax.all_gather(values, "tok", axis=0, tiled=True)
    row_count = key_part.shape[0]
    step_rows = math.gcd(row_count, 512)
    key_grid = key_part.reshape(row_count, kv_local, HD)
    value_grid = value_part.reshape(row_count, kv_local, HD)

    def advance(step_index, status):
        offset = step_index * step_rows
        key_pos = key_positions(offset, step_rows)

        def update(current):
            running, denominator, weighted = current
            key_block = lax.dynamic_slice_in_dim(key_grid, offset, step_rows, 0)
            value_block = lax.dynamic_slice_in_dim(value_grid, offset, step_rows, 0)
            scores = (
                jnp.einsum(
                    "hqd,khd->hqk", query_grid, key_block, preferred_element_type=jnp.float32
                )
                * scale_factor
            )
            allowed = (key_pos[None, :] <= query_pos[:, None])[None]
            masked = jnp.where(allowed, scores, -1e30)
            highest = jnp.maximum(running, jnp.max(masked, axis=-1))
            expo_terms = jnp.where(allowed, jnp.exp(masked - highest[..., None]), 0.0)
            shrink = jnp.exp(running - highest)
            denominator = denominator * shrink + jnp.sum(expo_terms, axis=-1)
            weighted = weighted * shrink[..., None] + jnp.einsum(
                "hqk,khd->hqd",
                expo_terms.astype(jnp.bfloat16),
                value_block,
                preferred_element_type=jnp.float32,
            )
            return (highest, denominator, weighted)

        return lax.cond(jnp.min(key_pos) > last_row, lambda unchanged: unchanged, update, status)

    running, denominator, weighted = lax.fori_loop(0, row_count // step_rows, advance, initial)
    context = (
        (weighted / denominator[..., None])
        .reshape(kv_local, QPK, tok_rows, HD)
        .transpose(2, 0, 1, 3)
    )
    context = context.reshape(tok_rows, kv_local * QPK * HD).astype(jnp.bfloat16)
    return context


def project_out(context, w_out):
    partial_value = jnp.dot(
        context,
        lax.all_gather(w_out, "tok", axis=1, tiled=True),
        preferred_element_type=jnp.float32,
    )
    return lax.psum_scatter(
        partial_value.astype(jnp.bfloat16), "head", scatter_dimension=1, tiled=True
    )


def hand_over(prefill_cache, lengths, prefill_table, decode_table):
    tok_count = lax.axis_size("tok")
    my_index = lax.axis_index("tok")
    layers, slot_count, kv_local, extent = prefill_cache.shape
    block_total = prefill_table.shape[0]
    request_count = lengths.shape[0]
    per_request = block_total // request_count
    every_block = jnp.arange(block_total, dtype=jnp.int32)
    logical_of = jnp.zeros((block_total,), jnp.int32).at[prefill_table].set(every_block)
    held_here = lax.dynamic_slice_in_dim(logical_of, my_index * slot_count, slot_count)
    request = held_here // per_request
    request_len = jnp.sum(
        jnp.where(
            request[:, None] == jnp.arange(request_count, dtype=jnp.int32)[None, :],
            lengths[None, :],
            0,
        ),
        axis=1,
    )
    live_rows = (held_here % per_request * BLK)[:, None] + jnp.arange(BLK, dtype=jnp.int32)[
        None, :
    ] < request_len[:, None]
    masked = prefill_cache.reshape(layers, slot_count, kv_local, BLK, extent // BLK) * live_rows[
        None, :, None, :, None
    ].astype(jnp.bfloat16)
    masked = masked.reshape(layers, slot_count, kv_local, extent)
    target = decode_table[held_here] // slot_count
    send_order = jnp.argsort(target * slot_count + jnp.arange(slot_count, dtype=jnp.int32))
    outgoing = jnp.take(masked, send_order, axis=1)
    per_peer = slot_count // tok_count
    decode_of = jnp.zeros((block_total,), jnp.int32).at[decode_table].set(every_block)
    arriving = lax.dynamic_slice_in_dim(decode_of, my_index * slot_count, slot_count)
    anchor = prefill_table[arriving]
    position = jnp.argsort(jnp.argsort(anchor))
    collected = []
    for layer_index in range(layers):
        sending = outgoing[layer_index].reshape(tok_count, per_peer, kv_local, extent)
        received = lax.all_to_all(sending, "tok", split_axis=0, concat_axis=0, tiled=True)
        collected.append(received.reshape(slot_count, kv_local, extent))
    incoming = jnp.stack(collected)
    return jnp.take(incoming, position, axis=1)


def on_device(
    hidden_in, norm_gain, w_qkv, w_out, prefill_cache, lengths, prefill_table, decode_table
):
    context = attend(hidden_in, norm_gain, w_qkv)
    attn_out = project_out(context, w_out)
    decode_cache = hand_over(prefill_cache, lengths, prefill_table, decode_table)
    return (attn_out, decode_cache)


def solution(mesh):
    in_specs = (
        P("tok", None),
        P(),
        P("tok", "head"),
        P("head", "tok"),
        P(None, "tok", "head", None),
        P(),
        P(),
        P(),
    )
    out_specs = (P("tok", "head"), P(None, "tok", "head", None))
    return jax.shard_map(
        on_device, mesh=mesh, in_specs=in_specs, out_specs=out_specs, check_vma=False
    )
```

profile of v0, /device:TPU:64, one launch (start us, length us, event | category | flops | bytes accessed | tf_op | source)
XLA Modules:
  0.0 723.2 jit_solution(4846801455397867306)
XLA Ops:
  7.2 0.7 all-gather.6.cloned.1.call-update
  8.0 1.7 fusion.24
  9.7 124.3 %all-gather.6.cloned.1.call-done = bf16[2560,480]{1,0:T(8,128)(2,1)} async-done(((bf16[40,480]{1,0:T(8,128)(2,1)}), bf16[2560,480]{1,0:T(8,128)(2,1)}) %all-gather.6.cloned.1.call-update) | async-done | bytes 2457616 | tf_op jit(solution)/shard_map/all_gather | solution.py:37
  134.0 3.4 fusion.27
  139.1 15.5 %scatter_custom_fusion = s32[4096]{0:T(1024)S(1)} fusion(s32[4096]{0:T(1024)S(1)} %compare_select_fusion.3, s32[4096]{0:T(1024)S(1)} %iota.52, s32[]{:T(128)} %copy.199), kind=kCustom, calls=%fused_computation.84 | custom fusion | bytes 16388 | tf_op jit(solution)/shard_map/scatter | solution.py:138
  154.6 15.5 %scatter_custom_fusion.1 = s32[4096]{0:T(1024)S(1)} fusion(s32[4096]{0:T(1024)S(1)} %compare_select_fusion.2, s32[4096]{0:T(1024)S(1)} %iota.55, s32[]{:T(128)} %copy.199), kind=kCustom, calls=%fused_computation.82 | custom fusion | bytes 16388 | tf_op jit(solution)/shard_map/scatter | solution.py:160
  171.0 0.8 gather_fusion
  171.7 2.0 sort.45
  173.8 0.8 fusion.29
  175.5 2.4 slice_bitcast_fusion
  178.5 1.6 reduce.4
  180.1 0.7 reshape.360
  180.8 10.3 %all-to-all-start = ((bf16[64,2,640]{2,1,0:T(2,128)(2,1)}), bf16[64,2,640]{2,1,0:T(2,128)(2,1)S(1)}, u32[]{:S(2)}, u32[]{:S(2)}) async-start(bf16[64,2,640]{2,1,0:T(2,128)(2,1)} %reshape.360), calls=%async_computation.1 | async-start | bytes 327680 | tf_op jit(solution)/shard_map/all_to_all | solution.py:167
  191.1 1.6 reduce.5
  192.8 0.7 reshape.362
  193.5 17.4 %all-to-all-done = bf16[64,2,640]{2,1,0:T(2,128)(2,1)S(1)} async-done(((bf16[64,2,640]{2,1,0:T(2,128)(2,1)}), bf16[64,2,640]{2,1,0:T(2,128)(2,1)S(1)}, u32[]{:S(2)}, u32[]{:S(2)}) %all-to-all-start) | async-done | bytes 163872 | tf_op jit(solution)/shard_map/all_to_all | solution.py:167
  210.8 6.8 all-to-all-start.1
  218.2 1.6 reduce.6
  219.8 0.7 reshape.364
  220.8 22.2 %all-to-all-done.1 = bf16[64,2,640]{2,1,0:T(2,128)(2,1)S(1)} async-done(((bf16[64,2,640]{2,1,0:T(2,128)(2,1)}), bf16[64,2,640]{2,1,0:T(2,128)(2,1)S(1)}, u32[]{:S(2)}, u32[]{:S(2)}) %all-to-all-start.1) | async-done | bytes 163872 | tf_op jit(solution)/shard_map/all_to_all | solution.py:167
  242.9 4.6 all-to-all-start.2
  248.2 1.6 reduce.7
  249.8 0.7 reshape.366
  250.5 1.6 reduce.8
  252.2 0.7 reshape.368
  253.2 13.7 %all-to-all-done.2 = bf16[64,2,640]{2,1,0:T(2,128)(2,1)S(1)} async-done(((bf16[64,2,640]{2,1,0:T(2,128)(2,1)}), bf16[64,2,640]{2,1,0:T(2,128)(2,1)S(1)}, u32[]{:S(2)}, u32[]{:S(2)}) %all-to-all-start.2) | async-done | bytes 163872 | tf_op jit(solution)/shard_map/all_to_all | solution.py:167
  266.9 14.7 %all-to-all-start.3 = ((bf16[64,2,640]{2,1,0:T(2,128)(2,1)}), bf16[64,2,640]{2,1,0:T(2,128)(2,1)S(1)}, u32[]{:S(2)}, u32[]{:S(2)}) async-start(bf16[64,2,640]{2,1,0:T(2,128)(2,1)} %reshape.366), calls=%async_computation.4 | async-start | bytes 327680 | tf_op jit(solution)/shard_map/all_to_all | solution.py:167
  281.6 3.3 all-gather.8.cloned.1.call-done
  284.9 130.3 %all-gather.12.cloned.1.call-done = bf16[16384,1,1,80]{0,3,2,1:T(8,128)(2,1)} async-done(((bf16[256,1,1,80]{0,3,2,1:T(8,128)(2,1)}), bf16[16384,1,1,80]{0,3,2,1:T(8,128)(2,1)}) %all-gather.12.cloned.1.call-update) | async-done | bytes 2621456 | tf_op jit(solution)/shard_map/all_gather | solution.py:73
  415.3 64.7 %while.18 = (s32[]{:T(128)}, f32[1,1024]{1,0:T(1,128)S(1)}, f32[1,1024]{1,0:T(1,128)S(1)}, f32[1,1024,80]{1,2,0:T(8,128)S(1)}, s32[]{:T(128)}, /*index=5*/bf16[1...) while((s32[]{:T(128)}, f32[1,1024]{1,0:T(1,128)S(1)}, ...), condition=%wide.region_8.9_spmd.clone, body=%wide.region_2.8_spmd.clone.sunk | while | flops 176327680 | bytes 7374129 | solution.py:109
  417.1 3.8 conditional.3
  417.2 1.4 fusion.2
  419.2 1.6 fusion.5
  420.9 0.7 iota_add_fusion.4
  422.8 0.7 iota_add_fusion.4
  424.8 0.7 iota_add_fusion.4
  434.3 0.7 iota_add_fusion.4
  436.2 0.7 iota_add_fusion.4
  438.1 0.7 iota_add_fusion.4
  443.8 0.7 iota_add_fusion.4
  445.7 0.7 iota_add_fusion.4
  453.3 0.7 iota_add_fusion.4
  480.0 137.3 %all-to-all-start.4 = ((bf16[64,2,640]{2,1,0:T(2,128)(2,1)}), bf16[64,2,640]{2,1,0:T(2,128)(2,1)S(1)}, u32[]{:S(2)}, u32[]{:S(2)}) async-start(bf16[64,2,640]{2,1,0:T(2,128)(2,1)} %reshape.368), calls=%async_computation.5 | async-start | bytes 327680 | tf_op jit(solution)/shard_map/all_to_all | solution.py:167
  617.6 3.4 convolution_convert_fusion
  621.1 1.6 reduce.9
  622.7 0.7 reshape.370
  623.4 12.6 %all-to-all-done.4 = bf16[64,2,640]{2,1,0:T(2,128)(2,1)S(1)} async-done(((bf16[64,2,640]{2,1,0:T(2,128)(2,1)}), bf16[64,2,640]{2,1,0:T(2,128)(2,1)S(1)}, u32[]{:S(2)}, u32[]{:S(2)}) %all-to-all-start.4) | async-done | bytes 163872 | tf_op jit(solution)/shard_map/all_to_all | solution.py:167
  636.0 5.1 all-to-all-start.5
  641.2 1.6 reduce.10
  642.8 0.7 reshape.372
  643.5 18.4 %all-to-all-done.5 = bf16[64,2,640]{2,1,0:T(2,128)(2,1)S(1)} async-done(((bf16[64,2,640]{2,1,0:T(2,128)(2,1)}), bf16[64,2,640]{2,1,0:T(2,128)(2,1)S(1)}, u32[]{:S(2)}, u32[]{:S(2)}) %all-to-all-start.5) | async-done | bytes 163872 | tf_op jit(solution)/shard_map/all_to_all | solution.py:167
  661.9 4.6 all-to-all-start.6
  666.5 1.6 reduce.11
  668.2 0.7 reshape.374
  668.9 15.6 %all-to-all-done.6 = bf16[64,2,640]{2,1,0:T(2,128)(2,1)S(1)} async-done(((bf16[64,2,640]{2,1,0:T(2,128)(2,1)}), bf16[64,2,640]{2,1,0:T(2,128)(2,1)S(1)}, u32[]{:S(2)}, u32[]{:S(2)}) %all-to-all-start.6) | async-done | bytes 163872 | tf_op jit(solution)/shard_map/all_to_all | solution.py:167
  684.5 4.6 all-to-all-start.7
  689.1 0.8 gather_fusion.1
  689.9 2.0 sort.46
  691.9 2.0 sort.47
  694.8 0.8 reshape.373
  695.6 11.5 %all-to-all-done.7 = bf16[64,2,640]{2,1,0:T(2,128)(2,1)S(1)} async-done(((bf16[64,2,640]{2,1,0:T(2,128)(2,1)}), bf16[64,2,640]{2,1,0:T(2,128)(2,1)S(1)}, u32[]{:S(2)}, u32[]{:S(2)}) %all-to-all-start.7) | async-done | bytes 163872 | tf_op jit(solution)/shard_map/all_to_all | solution.py:167
  707.1 0.9 reshape.375
  708.0 6.6 stack.3
  715.4 1.3 copy.174
  (195 shorter events, 24.5 us)
Async XLA Ops:
  7.2 126.8 %all-gather.6.cloned.1.call-start = ((), (), s32[]{:S(2)}) async-start(), calls=%async_computation.9 | async-start | bytes 2662400 | tf_op jit(solution)/shard_map/all_gather | solution.py:37
  7.9 277.0 %all-gather.8.cloned.1.call-start = ((), (), s32[]{:S(2)}) async-start(), calls=%async_computation.10 | async-start | bytes 2662400 | tf_op jit(solution)/shard_map/all_gather | solution.py:72
  9.6 129.4 %copy-start.1 = (s32[4096]{0:T(1024)S(1)}, s32[4096]{0:T(1024)}, u32[]{:S(2)}) copy-start(s32[4096]{0:T(1024)} %param.20) | copy-start | bytes 49156
  9.7 145.0 %copy-start = (s32[4096]{0:T(1024)S(1)}, s32[4096]{0:T(1024)}, u32[]{:S(2)}) copy-start(s32[4096]{0:T(1024)} %param.21) | copy-start | bytes 49156
  9.7 160.7 %copy-start.3 = (s32[8]{0:T(128)S(1)}, s32[8]{0:T(128)}, u32[]{:S(2)}) copy-start(s32[8]{0:T(128)} %param.19) | copy-start | bytes 100
  137.4 36.4 %copy-start.2 = (bf16[8,64,1,1280]{3,1,2,0:T(8,128)(2,1)S(1)}, bf16[8,64,1,1280]{3,1,2,0:T(8,128)(2,1)}, u32[]{:S(2)}) copy-start(bf16[8,64,1,1280]{3,1,2,0:T(8,128)(2,1)} %param.18) | copy-start | bytes 3932164
  138.3 276.9 %all-gather.12.cloned.1.call-start = ((), (), s32[]{:S(2)}) async-start(), calls=%async_computation.13 | async-start | bytes 2662400 | tf_op jit(solution)/shard_map/all_gather | solution.py:73
  180.8 30.0 %all-to-all-start = ((bf16[64,2,640]{2,1,0:T(2,128)(2,1)}), bf16[64,2,640]{2,1,0:T(2,128)(2,1)S(1)}, u32[]{:S(2)}, u32[]{:S(2)}) async-start(bf16[64,2,640]{2,1,0:T(2,128)(2,1)} %reshape.360), calls=%async_computation.1 | async-start | bytes 327680 | tf_op jit(solution)/shard_map/all_to_all | solution.py:167
  210.8 32.1 %all-to-all-start.1 = ((bf16[64,2,640]{2,1,0:T(2,128)(2,1)}), bf16[64,2,640]{2,1,0:T(2,128)(2,1)S(1)}, u32[]{:S(2)}, u32[]{:S(2)}) async-start(bf16[64,2,640]{2,1,0:T(2,128)(2,1)} %reshape.362), calls=%async_computation.2 | async-start | bytes 327680 | tf_op jit(solution)/shard_map/all_to_all | solution.py:167
  217.6 400.0 %all-gather.10.cloned.1.call-start = ((), (), s32[]{:S(2)}) async-start(), calls=%async_computation.11 | async-start | bytes 1996800 | tf_op jit(solution)/shard_map/all_gather | solution.py:122
  242.9 23.9 %all-to-all-start.2 = ((bf16[64,2,640]{2,1,0:T(2,128)(2,1)}), bf16[64,2,640]{2,1,0:T(2,128)(2,1)S(1)}, u32[]{:S(2)}, u32[]{:S(2)}) async-start(bf16[64,2,640]{2,1,0:T(2,128)(2,1)} %reshape.364), calls=%async_computation.3 | async-start | bytes 327680 | tf_op jit(solution)/shard_map/all_to_all | solution.py:167
  266.9 213.1 %all-to-all-start.3 = ((bf16[64,2,640]{2,1,0:T(2,128)(2,1)}), bf16[64,2,640]{2,1,0:T(2,128)(2,1)S(1)}, u32[]{:S(2)}, u32[]{:S(2)}) async-start(bf16[64,2,640]{2,1,0:T(2,128)(2,1)} %reshape.366), calls=%async_computation.4 | async-start | bytes 327680 | tf_op jit(solution)/shard_map/all_to_all | solution.py:167
  480.0 156.0 %all-to-all-start.4 = ((bf16[64,2,640]{2,1,0:T(2,128)(2,1)}), bf16[64,2,640]{2,1,0:T(2,128)(2,1)S(1)}, u32[]{:S(2)}, u32[]{:S(2)}) async-start(bf16[64,2,640]{2,1,0:T(2,128)(2,1)} %reshape.368), calls=%async_computation.5 | async-start | bytes 327680 | tf_op jit(solution)/shard_map/all_to_all | solution.py:167
  617.3 99.3 %reduce-scatter.2.cloned.1.call-start = ((), (), s32[]{:S(2)}) async-start(), calls=%async_computation.12 | async-start | bytes 1474560 | tf_op jit(solution)/shard_map/reduce_scatter | solution.py:125
  636.0 25.9 %all-to-all-start.5 = ((bf16[64,2,640]{2,1,0:T(2,128)(2,1)}), bf16[64,2,640]{2,1,0:T(2,128)(2,1)S(1)}, u32[]{:S(2)}, u32[]{:S(2)}) async-start(bf16[64,2,640]{2,1,0:T(2,128)(2,1)} %reshape.370), calls=%async_computation.6 | async-start | bytes 327680 | tf_op jit(solution)/shard_map/all_to_all | solution.py:167
  661.9 22.6 %all-to-all-start.6 = ((bf16[64,2,640]{2,1,0:T(2,128)(2,1)}), bf16[64,2,640]{2,1,0:T(2,128)(2,1)S(1)}, u32[]{:S(2)}, u32[]{:S(2)}) async-start(bf16[64,2,640]{2,1,0:T(2,128)(2,1)} %reshape.372), calls=%async_computation.7 | async-start | bytes 327680 | tf_op jit(solution)/shard_map/all_to_all | solution.py:167
  684.5 22.6 %all-to-all-start.7 = ((bf16[64,2,640]{2,1,0:T(2,128)(2,1)}), bf16[64,2,640]{2,1,0:T(2,128)(2,1)S(1)}, u32[]{:S(2)}, u32[]{:S(2)}) async-start(bf16[64,2,640]{2,1,0:T(2,128)(2,1)} %reshape.374), calls=%async_computation.8 | async-start | bytes 327680 | tf_op jit(solution)/shard_map/all_to_all | solution.py:167
Sparse Core Ops, SparseCore 0:
  12.2 121.7 all-gather.5
  138.4 146.4 all-gather.7
  288.9 126.2 all-gather.11
  419.3 116.7 all-gather.9
  621.2 42.9 reduce-scatter.1
where the time goes:
time: 727 us; the launch traced here: 723 us
  waiting for transfers between devices  370 us (51%)
  starting transfers between devices  188 us (26%)
  local copies, waits for them, and re-layouts  54.5 us (7%)
  other arithmetic  46 us (6%)
  loops' own time  39.5 us (5%)
  between operations  14.3 us (2%)
  matrix products  9.89 us (1%)
    all_to_all x8, starting transfers between devices, hand_over(): lax.all_to_all(sending, 'tok', split_axis=0, concat_axis=0, tiled=True)  188 us
    all_gather x1, waiting for transfers between devices, attend(): value_part = lax.all_gather(values, 'tok', axis=0, tiled=True)  130 us
    all_gather x1, waiting for transfers between devices, attend(): lax.all_gather(w_qkv, 'tok', axis=0, tiled=True)  124 us
    all_to_all x8, waiting for transfers between devices, hand_over(): lax.all_to_all(sending, 'tok', split_axis=0, concat_axis=0, tiled=True)  111 us
    another operation x1, loops' own time, attend(): lax.fori_loop(0, row_count // step_rows, advance, initial)  38.6 us
    add x32, other arithmetic, key_positions(): whole_rows = block_start + jnp.arange(count, dtype=jnp.int32)  21.3 us
    scatter x1, local copies, waits for them, and re-layouts, hand_over(): jnp.zeros((block_total,), jnp.int32).at[decode_table].set(every_block)  15.5 us
    scatter x1, local copies, waits for them, and re-layouts, hand_over(): jnp.zeros((block_total,), jnp.int32).at[prefill_table].set(every_block)  15.5 us
  transfers between devices with their start and end apart: 13, of which 10 were waited for; matrix products, arithmetic and copies ran while one was open for 15% of the time, Pallas kernels for 0%

commit v1 on v0

--- a/solution.py
+++ b/solution.py
@@ -34,7 +34,11 @@
         * norm_gain
     ).astype(jnp.bfloat16)
     projected = jnp.dot(
-        normed, lax.all_gather(w_qkv, "tok", axis=0, tiled=True), preferred_element_type=jnp.float32
+        normed,
+        jnp.concatenate(
+            lax.all_to_all(jnp.stack([w_qkv] * lax.axis_size("tok")), "tok", 0, 0), axis=0
+        ),
+        preferred_element_type=jnp.float32,
     )
     kv_local = w_qkv.shape[1] // ((QPK + 2) * HD)
     projected = projected.reshape(tok_rows, kv_local, QPK + 2, HD)

time: 727 us -> 741 us (1.019)
  starting transfers between devices: 188 us -> 199 us
    all_gather x1 -> x0, waiting for transfers between devices: 124 us -> none  [attend(): lax.all_gather(w_qkv, 'tok', axis=0, tiled=True)]
    all_to_all x0 -> x1, waiting for transfers between devices: none -> 120 us  [attend(): lax.all_to_all(jnp.stack([w_qkv] * lax.axis_size('tok')), 'tok', 0, 0)]
    all_to_all x0 -> x1, starting transfers between devices: none -> 19.4 us  [attend(): lax.all_to_all(jnp.stack([w_qkv] * lax.axis_size('tok')), 'tok', 0, 0)]
    all_to_all x8, waiting for transfers between devices: 111 us -> 123 us  [hand_over(): lax.all_to_all(sending, 'tok', split_axis=0, concat_axis=0, tiled=True)]
    all_to_all x8, starting transfers between devices: 188 us -> 179 us  [hand_over(): lax.all_to_all(sending, 'tok', split_axis=0, concat_axis=0, tiled=True)]
    all_gather x1, waiting for transfers between devices: 130 us -> 122 us  [attend(): value_part = lax.all_gather(values, 'tok', axis=0, tiled=True)]
  transfers between devices with their start and end apart: 13 -> 13, of which waited for: 10 -> 9; matrix products, arithmetic and copies ran while one was open for 15% -> 15% of each run, Pallas kernels for 0% -> 0%
where the time goes in v1:
time: 741 us; the launch traced here: 737 us
  waiting for transfers between devices  367 us (50%)
  starting transfers between devices  199 us (27%)
  local copies, waits for them, and re-layouts  59.6 us (8%)
  other arithmetic  47.7 us (6%)
  loops' own time  39.5 us (5%)
  between operations  14.2 us (2%)
  matrix products  9.55 us (1%)
    all_to_all x8, starting transfers between devices, hand_over(): lax.all_to_all(sending, 'tok', split_axis=0, concat_axis=0, tiled=True)  179 us
    all_to_all x8, waiting for transfers between devices, hand_over(): lax.all_to_all(sending, 'tok', split_axis=0, concat_axis=0, tiled=True)  123 us
    all_gather x1, waiting for transfers between devices, attend(): value_part = lax.all_gather(values, 'tok', axis=0, tiled=True)  122 us
    all_to_all x1, waiting for transfers between devices, attend(): lax.all_to_all(jnp.stack([w_qkv] * lax.axis_size('tok')), 'tok', 0, 0)  120 us
    another operation x1, loops' own time, attend(): lax.fori_loop(0, row_count // step_rows, advance, initial)  38.6 us
    add x32, other arithmetic, key_positions(): whole_rows = block_start + jnp.arange(count, dtype=jnp.int32)  21.3 us
    all_to_all x1, starting transfers between devices, attend(): lax.all_to_all(jnp.stack([w_qkv] * lax.axis_size('tok')), 'tok', 0, 0)  19.4 us
    scatter x1, local copies, waits for them, and re-layouts, hand_over(): jnp.zeros((block_total,), jnp.int32).at[prefill_table].set(every_block)  15.5 us
  transfers between devices with their start and end apart: 13, of which 9 were waited for; matrix products, arithmetic and copies ran while one was open for 15% of the time, Pallas kernels for 0%

profile of v1, /device:TPU:64, one launch (start us, length us, event | category | flops | bytes accessed | tf_op | source)
XLA Modules:
  0.0 736.7 jit_solution(1561148487673639273)
XLA Ops:
  7.2 2.5 stack.4
  9.6 19.4 %all-to-all-start = ((bf16[64,40,480]{2,1,0:T(8,128)(2,1)}), bf16[64,40,480]{2,1,0:T(8,128)(2,1)S(1)}, u32[]{:S(2)}, u32[]{:S(2)}) async-start(bf16[64,40,480]{2,1,0:T(8,128)(2,1)} %stack.4), calls=%async_computation | async-start | bytes 5242880 | tf_op jit(solution)/shard_map/all_to_all | solution.py:39
  29.1 1.7 fusion.24
  30.8 120.5 %all-to-all-done = bf16[64,40,480]{2,1,0:T(8,128)(2,1)S(1)} async-done(((bf16[64,40,480]{2,1,0:T(8,128)(2,1)}), bf16[64,40,480]{2,1,0:T(8,128)(2,1)S(1)}, u32[]{:S(2)}, u32[]{:S(2)}) %all-to-all-start) | async-done | bytes 2457632 | tf_op jit(solution)/shard_map/all_to_all | solution.py:39
  151.3 2.7 copy.167
  154.0 3.0 fusion.33
  158.7 15.5 %scatter_custom_fusion = s32[4096]{0:T(1024)S(1)} fusion(s32[4096]{0:T(1024)S(1)} %compare_select_fusion.3, s32[4096]{0:T(1024)S(1)} %iota.52, s32[]{:T(128)} %copy.214), kind=kCustom, calls=%fused_computation.86 | custom fusion | bytes 16388 | tf_op jit(solution)/shard_map/scatter | solution.py:142
  174.3 15.5 %scatter_custom_fusion.1 = s32[4096]{0:T(1024)S(1)} fusion(s32[4096]{0:T(1024)S(1)} %compare_select_fusion.2, s32[4096]{0:T(1024)S(1)} %iota.55, s32[]{:T(128)} %copy.214), kind=kCustom, calls=%fused_computation.84 | custom fusion | bytes 16388 | tf_op jit(solution)/shard_map/scatter | solution.py:164
  190.6 0.8 gather_fusion
  191.4 2.0 sort.45
  193.4 2.1 fusion.30
  196.4 2.4 slice_bitcast_fusion
  199.4 1.7 reduce.4
  201.1 0.7 reshape.371
  201.8 7.7 %all-to-all-start.1 = ((bf16[64,2,640]{2,1,0:T(2,128)(2,1)}), bf16[64,2,640]{2,1,0:T(2,128)(2,1)S(1)}, u32[]{:S(2)}, u32[]{:S(2)}) async-start(bf16[64,2,640]{2,1,0:T(2,128)(2,1)} %reshape.371), calls=%async_computation.2 | async-start | bytes 327680 | tf_op jit(solution)/shard_map/all_to_all | solution.py:171
  209.5 1.7 reduce.5
  211.2 0.7 reshape.373
  211.9 18.2 %all-to-all-done.1 = bf16[64,2,640]{2,1,0:T(2,128)(2,1)S(1)} async-done(((bf16[64,2,640]{2,1,0:T(2,128)(2,1)}), bf16[64,2,640]{2,1,0:T(2,128)(2,1)S(1)}, u32[]{:S(2)}, u32[]{:S(2)}) %all-to-all-start.1) | async-done | bytes 163872 | tf_op jit(solution)/shard_map/all_to_all | solution.py:171
  230.0 6.5 all-to-all-start.2
  236.6 0.7 all-gather.7.cloned.1.call-update
  237.3 1.7 reduce.6
  238.9 0.7 reshape.375
  239.9 27.7 %all-to-all-done.2 = bf16[64,2,640]{2,1,0:T(2,128)(2,1)S(1)} async-done(((bf16[64,2,640]{2,1,0:T(2,128)(2,1)}), bf16[64,2,640]{2,1,0:T(2,128)(2,1)S(1)}, u32[]{:S(2)}, u32[]{:S(2)}) %all-to-all-start.2) | async-done | bytes 163872 | tf_op jit(solution)/shard_map/all_to_all | solution.py:171
  267.6 6.3 all-to-all-start.3
  274.5 1.7 reduce.7
  276.1 0.7 reshape.377
  276.9 1.7 reduce.8
  278.5 0.7 reshape.379
  279.5 19.8 %all-to-all-done.3 = bf16[64,2,640]{2,1,0:T(2,128)(2,1)S(1)} async-done(((bf16[64,2,640]{2,1,0:T(2,128)(2,1)}), bf16[64,2,640]{2,1,0:T(2,128)(2,1)S(1)}, u32[]{:S(2)}, u32[]{:S(2)}) %all-to-all-start.3) | async-done | bytes 163872 | tf_op jit(solution)/shard_map/all_to_all | solution.py:171
  299.4 7.4 all-to-all-start.4
  306.7 122.2 %all-gather.9.cloned.1.call-done = bf16[16384,1,1,80]{0,3,2,1:T(8,128)(2,1)} async-done(((bf16[256,1,1,80]{0,3,2,1:T(8,128)(2,1)}), bf16[16384,1,1,80]{0,3,2,1:T(8,128)(2,1)}) %all-gather.9.cloned.1.call-update) | async-done | bytes 2621456 | tf_op jit(solution)/shard_map/all_gather | solution.py:77
  429.0 64.7 %while.18 = (s32[]{:T(128)}, f32[1,1024]{1,0:T(1,128)S(1)}, f32[1,1024]{1,0:T(1,128)S(1)}, f32[1,1024,80]{1,2,0:T(8,128)S(1)}, s32[]{:T(128)}, /*index=5*/bf16[1...) while((s32[]{:T(128)}, f32[1,1024]{1,0:T(1,128)S(1)}, ...), condition=%wide.region_8.9_spmd.clone, body=%wide.region_2.8_spmd.clone.sunk | while | flops 176327680 | bytes 7374129 | solution.py:113
  430.9 3.8 conditional.3
  430.9 1.4 fusion.2
  433.0 1.6 fusion.5
  434.7 0.7 iota_add_fusion.4
  436.6 0.7 iota_add_fusion.4
  444.2 0.7 iota_add_fusion.4
  446.2 0.7 iota_add_fusion.4
  448.1 0.7 iota_add_fusion.4
  455.7 0.7 iota_add_fusion.4
  457.6 0.7 iota_add_fusion.4
  493.8 137.3 %all-to-all-start.5 = ((bf16[64,2,640]{2,1,0:T(2,128)(2,1)}), bf16[64,2,640]{2,1,0:T(2,128)(2,1)S(1)}, u32[]{:S(2)}, u32[]{:S(2)}) async-start(bf16[64,2,640]{2,1,0:T(2,128)(2,1)} %reshape.379), calls=%async_computation.6 | async-start | bytes 327680 | tf_op jit(solution)/shard_map/all_to_all | solution.py:171
  631.4 3.4 convolution_convert_fusion
  634.8 1.7 reduce.9
  636.5 0.7 reshape.381
  637.2 12.6 %all-to-all-done.5 = bf16[64,2,640]{2,1,0:T(2,128)(2,1)S(1)} async-done(((bf16[64,2,640]{2,1,0:T(2,128)(2,1)}), bf16[64,2,640]{2,1,0:T(2,128)(2,1)S(1)}, u32[]{:S(2)}, u32[]{:S(2)}) %all-to-all-start.5) | async-done | bytes 163872 | tf_op jit(solution)/shard_map/all_to_all | solution.py:171
  649.8 5.2 all-to-all-start.6
  655.0 1.7 reduce.10
  656.6 0.7 reshape.383
  657.4 18.4 %all-to-all-done.6 = bf16[64,2,640]{2,1,0:T(2,128)(2,1)S(1)} async-done(((bf16[64,2,640]{2,1,0:T(2,128)(2,1)}), bf16[64,2,640]{2,1,0:T(2,128)(2,1)S(1)}, u32[]{:S(2)}, u32[]{:S(2)}) %all-to-all-start.6) | async-done | bytes 163872 | tf_op jit(solution)/shard_map/all_to_all | solution.py:171
  675.8 4.6 all-to-all-start.7
  680.4 1.7 reduce.11
  682.1 0.7 reshape.385
  682.8 15.3 %all-to-all-done.7 = bf16[64,2,640]{2,1,0:T(2,128)(2,1)S(1)} async-done(((bf16[64,2,640]{2,1,0:T(2,128)(2,1)}), bf16[64,2,640]{2,1,0:T(2,128)(2,1)S(1)}, u32[]{:S(2)}, u32[]{:S(2)}) %all-to-all-start.7) | async-done | bytes 163872 | tf_op jit(solution)/shard_map/all_to_all | solution.py:171
  698.0 4.6 all-to-all-start.8
  702.7 0.8 gather_fusion.1
  703.5 2.0 sort.46
  705.5 2.0 sort.47
  708.3 0.8 reshape.384
  709.2 11.5 %all-to-all-done.8 = bf16[64,2,640]{2,1,0:T(2,128)(2,1)S(1)} async-done(((bf16[64,2,640]{2,1,0:T(2,128)(2,1)}), bf16[64,2,640]{2,1,0:T(2,128)(2,1)S(1)}, u32[]{:S(2)}, u32[]{:S(2)}) %all-to-all-start.8) | async-done | bytes 163872 | tf_op jit(solution)/shard_map/all_to_all | solution.py:171
  720.6 0.9 reshape.386
  721.5 6.6 stack.5
  728.9 1.3 copy.189
  (196 shorter events, 25.3 us)
Async XLA Ops:
  9.6 141.6 %all-to-all-start = ((bf16[64,40,480]{2,1,0:T(8,128)(2,1)}), bf16[64,40,480]{2,1,0:T(8,128)(2,1)S(1)}, u32[]{:S(2)}, u32[]{:S(2)}) async-start(bf16[64,40,480]{2,1,0:T(8,128)(2,1)} %stack.4), calls=%async_computation | async-start | bytes 5242880 | tf_op jit(solution)/shard_map/all_to_all | solution.py:39
  29.0 277.7 %all-gather.5.cloned.1.call-start = ((), (), s32[]{:S(2)}) async-start(), calls=%async_computation.10 | async-start | bytes 2662400 | tf_op jit(solution)/shard_map/all_gather | solution.py:76
  151.3 2.7 copy-start.2
  154.0 4.7 copy-start.1
  154.0 20.3 %copy-start = (s32[4096]{0:T(1024)S(1)}, s32[4096]{0:T(1024)}, u32[]{:S(2)}) copy-start(s32[4096]{0:T(1024)} %param.21) | copy-start | bytes 49156
  154.0 36.0 %copy-start.3 = (s32[8]{0:T(128)S(1)}, s32[8]{0:T(128)}, u32[]{:S(2)}) copy-start(s32[8]{0:T(128)} %param.19) | copy-start | bytes 100
  157.9 271.1 %all-gather.9.cloned.1.call-start = ((), (), s32[]{:S(2)}) async-start(), calls=%async_computation.13 | async-start | bytes 2662400 | tf_op jit(solution)/shard_map/all_gather | solution.py:77
  201.8 28.2 %all-to-all-start.1 = ((bf16[64,2,640]{2,1,0:T(2,128)(2,1)}), bf16[64,2,640]{2,1,0:T(2,128)(2,1)S(1)}, u32[]{:S(2)}, u32[]{:S(2)}) async-start(bf16[64,2,640]{2,1,0:T(2,128)(2,1)} %reshape.371), calls=%async_computation.2 | async-start | bytes 327680 | tf_op jit(solution)/shard_map/all_to_all | solution.py:171
  230.0 37.6 %all-to-all-start.2 = ((bf16[64,2,640]{2,1,0:T(2,128)(2,1)}), bf16[64,2,640]{2,1,0:T(2,128)(2,1)S(1)}, u32[]{:S(2)}, u32[]{:S(2)}) async-start(bf16[64,2,640]{2,1,0:T(2,128)(2,1)} %reshape.373), calls=%async_computation.3 | async-start | bytes 327680 | tf_op jit(solution)/shard_map/all_to_all | solution.py:171
  236.5 394.8 %all-gather.7.cloned.1.call-start = ((), (), s32[]{:S(2)}) async-start(), calls=%async_computation.11 | async-start | bytes 1996800 | tf_op jit(solution)/shard_map/all_gather | solution.py:126
  267.6 31.8 %all-to-all-start.3 = ((bf16[64,2,640]{2,1,0:T(2,128)(2,1)}), bf16[64,2,640]{2,1,0:T(2,128)(2,1)S(1)}, u32[]{:S(2)}, u32[]{:S(2)}) async-start(bf16[64,2,640]{2,1,0:T(2,128)(2,1)} %reshape.375), calls=%async_computation.4 | async-start | bytes 327680 | tf_op jit(solution)/shard_map/all_to_all | solution.py:171
  299.4 194.4 %all-to-all-start.4 = ((bf16[64,2,640]{2,1,0:T(2,128)(2,1)}), bf16[64,2,640]{2,1,0:T(2,128)(2,1)S(1)}, u32[]{:S(2)}, u32[]{:S(2)}) async-start(bf16[64,2,640]{2,1,0:T(2,128)(2,1)} %reshape.377), calls=%async_computation.5 | async-start | bytes 327680 | tf_op jit(solution)/shard_map/all_to_all | solution.py:171
  493.8 156.0 %all-to-all-start.5 = ((bf16[64,2,640]{2,1,0:T(2,128)(2,1)}), bf16[64,2,640]{2,1,0:T(2,128)(2,1)S(1)}, u32[]{:S(2)}, u32[]{:S(2)}) async-start(bf16[64,2,640]{2,1,0:T(2,128)(2,1)} %reshape.379), calls=%async_computation.6 | async-start | bytes 327680 | tf_op jit(solution)/shard_map/all_to_all | solution.py:171
  631.1 99.1 %reduce-scatter.2.cloned.1.call-start = ((), (), s32[]{:S(2)}) async-start(), calls=%async_computation.12 | async-start | bytes 1474560 | tf_op jit(solution)/shard_map/reduce_scatter | solution.py:129
  649.8 26.0 %all-to-all-start.6 = ((bf16[64,2,640]{2,1,0:T(2,128)(2,1)}), bf16[64,2,640]{2,1,0:T(2,128)(2,1)S(1)}, u32[]{:S(2)}, u32[]{:S(2)}) async-start(bf16[64,2,640]{2,1,0:T(2,128)(2,1)} %reshape.381), calls=%async_computation.7 | async-start | bytes 327680 | tf_op jit(solution)/shard_map/all_to_all | solution.py:171
  675.8 22.3 %all-to-all-start.7 = ((bf16[64,2,640]{2,1,0:T(2,128)(2,1)}), bf16[64,2,640]{2,1,0:T(2,128)(2,1)S(1)}, u32[]{:S(2)}, u32[]{:S(2)}) async-start(bf16[64,2,640]{2,1,0:T(2,128)(2,1)} %reshape.383), calls=%async_computation.8 | async-start | bytes 327680 | tf_op jit(solution)/shard_map/all_to_all | solution.py:171
  698.0 22.6 %all-to-all-start.8 = ((bf16[64,2,640]{2,1,0:T(2,128)(2,1)}), bf16[64,2,640]{2,1,0:T(2,128)(2,1)S(1)}, u32[]{:S(2)}, u32[]{:S(2)}) async-start(bf16[64,2,640]{2,1,0:T(2,128)(2,1)} %reshape.385), calls=%async_computation.9 | async-start | bytes 327680 | tf_op jit(solution)/shard_map/all_to_all | solution.py:171
Sparse Core Ops, SparseCore 0:
  158.0 145.8 all-gather.4
  307.9 121.0 all-gather.8
  433.2 113.8 all-gather.6
  635.0 42.9 reduce-scatter.1
